TPU v7x, 128 devices: a whole 4x4x4 slice. The times are simulated.
128 devices in a mesh: lat: 8 (over z, core), lon: 16 (over y, x).
Axes of the slice: x: 4, y: 4, z: 4, core: 2. Of those that a mesh axis runs over, the one named last changes fastest.
Arguments:
- sigma: float32 [4, 1024, 2048], P(None, 'lat', 'lon'), may hold values from 0.5 to 2
- east_coef: float32 [4, 1024, 2048], P(None, 'lat', 'lon'), may hold values from 0.04 to 0.24
- north_coef: float32 [4, 1024, 2048], P(None, 'lat', 'lon'), may hold values from 0.04 to 0.24
- mask: int32 [4, 1024, 2048], P(None, 'lat', 'lon'), may hold values 0 or 1
- innovations: float32 [16384, 128], P(('lat', 'lon')), may hold values from -6 to 6
- cells: int32 [16384, 128], P(('lat', 'lon')), may hold values from 0 to 65535
- owner: int32 [16384, 1], P(('lat', 'lon')), may hold values from 0 to 127; in each aligned block of 128 rows (0 to 127, 128 to 255, ...) at most 2 rows name the same one
- obs_weights: float32 [16384, 128, 128], P(('lat', 'lon')), may hold values from 0 to 4, as said below
Outputs:
- increment: float32 [4, 1024, 2048], P(None, 'lat', 'lon')
- residual: float32 [4, 1024, 2048], P(None, 'lat', 'lon')
Inputs may be any that keep to these rules, and one draw needn't show every extreme that they name: `owner`: within the 128 blocks held by one device, no tile is named by more than 2 blocks, a bound that some block reaches. `obs_weights`: each block is symmetric and positive definite.
All inputs are finite; a program needn't handle non-finite values. No bound on the sum of `mask` on one device may be relied on, other than what follows from the above.
Results may differ from a plain program's by a relative error of at most 0.0003.
Values sent between devices are 32-bit elements; how exact they have to be, the bound alone decides.
A program may use at most 128 MiB of HBM per device.

v0:
```python
import jax
import jax.numpy as jnp
from jax import lax
from jax.sharding import PartitionSpec as P

PASSES = 5
ITERS = 2


def with_halo(block, sides, width):
    for axis, dim in sides:
        count = lax.axis_size(axis)
        forward = [(i, i + 1) for i in range(count - 1)]
        forward.append((count - 1, 0))
        backward = [(target, source) for source, target in forward]
        low = lax.ppermute(
            lax.slice_in_dim(block, block.shape[dim] - width, None, axis=dim), axis, forward
        )
        high = lax.ppermute(lax.slice_in_dim(block, 0, width, axis=dim), axis, backward)
        block = jnp.concatenate([low, block, high], axis=dim)
    return block


def face_tables(mask, east_coef, north_coef):
    stacked = jnp.stack([mask.astype(jnp.float32), east_coef, north_coef])
    padded = with_halo(stacked, (("lat", 2), ("lon", 3)), PASSES)
    tile_rows = mask.shape[1]
    global_rows = (
        lax.axis_index("lat") * tile_rows
        + jnp.arange(tile_rows + 2 * PASSES, dtype=jnp.int32)
        - PASSES
    )
    inside = ((global_rows >= 0) & (global_rows < tile_rows * lax.axis_size("lat"))).astype(
        jnp.float32
    )
    land = padded[0] * inside[None, :, None]
    east_face = padded[1][:, :, :-1] * land[:, :, :-1] * land[:, :, 1:]
    north_face = padded[2][:, :-1, :] * land[:, :-1, :] * land[:, 1:, :]
    return (east_face, north_face)


def one_pass(padded_field, depth, east_face, north_face):
    tile_rows = east_face.shape[1] - 2 * PASSES
    tile_cols = east_face.shape[2] + 1 - 2 * PASSES
    start = PASSES - depth
    row_span = tile_rows + 2 * depth
    col_span = tile_cols + 2 * depth
    center = padded_field[:, 1:-1, 1:-1]
    east = east_face[:, start : start + row_span, start : start + col_span]
    west = east_face[:, start : start + row_span, start - 1 : start - 1 + col_span]
    north = north_face[:, start : start + row_span, start : start + col_span]
    south = north_face[:, start - 1 : start - 1 + row_span, start : start + col_span]
    result = (
        center
        + east * (padded_field[:, 1:-1, 2:] - center)
        + west * (padded_field[:, 1:-1, :-2] - center)
    )
    return (
        result
        + north * (padded_field[:, 2:, 1:-1] - center)
        + south * (padded_field[:, :-2, 1:-1] - center)
    )


def smooth(field, east_face, north_face):
    for sweep in range(PASSES):
        padded = with_halo(field, (("lat", 1), ("lon", 2)), 1)
        field = one_pass(padded, 0, east_face, north_face)
    return field


def squares(residual):
    return lax.psum(jnp.sum(residual * residual), ("lat", "lon"))


def body(sigma, east_coef, north_coef, mask, innovations, cells, owner, obs_weights):
    east_face, north_face = face_tables(mask, east_coef, north_coef)
    devices = lax.axis_size("lat") * lax.axis_size("lon")
    held = owner.shape[0]
    block_width = cells.shape[1]
    capacity = max(2, (2 * held + devices - 1) // devices)
    slots = devices * capacity
    target = owner[:, 0]
    order = jnp.arange(held, dtype=jnp.int32)
    before = (target[:, None] == target[None, :]) & (order[None, :] < order[:, None])
    slot_rank = jnp.sum(before.astype(jnp.int32), axis=1)
    position = target * capacity + slot_rank
    placing = (jnp.arange(slots, dtype=jnp.int32)[:, None] == position[None, :]).astype(jnp.float32)

    def to_slots(blocks):
        return jnp.dot(
            placing, blocks, precision=lax.Precision.HIGHEST, preferred_element_type=jnp.float32
        )

    outgoing = to_slots(cells.astype(jnp.float32)).astype(jnp.int32)
    incoming = lax.all_to_all(
        outgoing.reshape(devices, capacity, block_width),
        ("lat", "lon"),
        split_axis=0,
        concat_axis=0,
        tiled=True,
    )
    incoming = incoming.reshape(-1)
    tile_shape = sigma.shape
    tile_cols = tile_shape[2]
    tile_lines = tile_shape[0] * tile_shape[1]
    line_index = incoming // tile_cols
    column_hit = (incoming % tile_cols)[:, None] == jnp.arange(tile_cols, dtype=jnp.int32)[None, :]

    def adjoint(weighted):
        parcel = to_slots(weighted)
        arrived = lax.all_to_all(
            parcel.reshape(devices, capacity, block_width),
            ("lat", "lon"),
            split_axis=0,
            concat_axis=0,
            tiled=True,
        )
        spread = jnp.where(column_hit, arrived.reshape(-1)[:, None], 0.0)
        total = jnp.zeros((tile_lines, tile_cols), jnp.float32).at[line_index].add(spread)
        return total.reshape(tile_shape)

    def weigh(values):
        return jnp.einsum("kij,kj->ki", obs_weights, values, precision=lax.Precision.HIGHEST)

    right = smooth(sigma * adjoint(weigh(innovations)), east_face, north_face)
    solution = jnp.zeros_like(right)
    residual = right
    direction = right
    norm_now = squares(residual)
    for sweep in range(ITERS):
        hessian_field = sigma * smooth(direction, east_face, north_face)
        lines = hessian_field.reshape(tile_lines, tile_cols)[line_index]
        observe_values = jnp.sum(jnp.where(column_hit, lines, 0.0), axis=1)
        returned = lax.all_to_all(
            observe_values.reshape(devices, capacity, block_width),
            ("lat", "lon"),
            split_axis=0,
            concat_axis=0,
            tiled=True,
        )
        seen = jnp.dot(
            placing.T,
            returned.reshape(slots, block_width),
            precision=lax.Precision.HIGHEST,
            preferred_element_type=jnp.float32,
        )
        image = direction + smooth(sigma * adjoint(weigh(seen)), east_face, north_face)
        alpha = norm_now / lax.psum(jnp.sum(direction * image), ("lat", "lon"))
        solution = solution + alpha * direction
        residual = residual - alpha * image
        norm_next = squares(residual)
        direction = residual + norm_next / norm_now * direction
        norm_now = norm_next
    increment = sigma * smooth(solution, east_face, north_face)
    return (increment, residual)


def solution(mesh):
    return jax.shard_map(
        body,
        mesh=mesh,
        in_specs=(
            P(None, "lat", "lon"),
            P(None, "lat", "lon"),
            P(None, "lat", "lon"),
            P(None, "lat", "lon"),
            P(("lat", "lon"), None),
            P(("lat", "lon"), None),
            P(("lat", "lon"), None),
            P(("lat", "lon"), None, None),
        ),
        out_specs=(P(None, "lat", "lon"), P(None, "lat", "lon")),
        check_vma=False,
    )
```

profile of v0, /device:TPU:1, one launch (start us, length us, event | category | flops | bytes accessed | tf_op | source)
XLA Modules:
  0.0 1778.3 jit_solution(6935189005297970195)
XLA Ops:
  3.9 11.5 all-to-all-start
  20.6 15.3 fusion.461
  43.4 6.4 collective-permute-done.2
  54.7 7.1 all-to-all-start.1
  62.5 9.4 all-to-all-done.1
  71.9 195.0 %scatter_custom_fusion = f32[512,128]{1,0:T(8,128)S(1)} fusion(s32[32768]{0:T(1024)S(1)} %bitcast.97, f32[]{:T(128)} %constant.36.clone.1, f32[32768]{0:T(1024)S(1)} %bitcast.105, s32[32768]{0:T(1024)S(1)} %add_select_fusion), kind=kCustom, calls=%fused_computation.11 | custom fusion | flops 12582912 | bytes 525312 | tf_op jit(solution)/shard_map/scatter-add | solution.py:120
  267.3 28.8 %collective-permute-start.5 = (f32[4,1,128]{2,0,1:T(4,128)S(1)}, f32[4,1,128]{2,0,1:T(4,128)S(1)}, u32[]{:S(2)}, u32[]{:S(2)}) collective-permute-start(f32[4,1,128]{2,0,1:T(4,128)S(1)} %get-tuple-element.143), channel_id=1, source_target_pairs={{16,0},{32,16},{48,32},{64,48},{80,64},{96,80},{112,96},{0,112},{1... | collective-permute-start | bytes 6152 | tf_op jit(solution)/shard_map/ppermute | solution.py:19
  303.2 5.2 collective-permute-done.7
  342.5 5.0 collective-permute-start.17
  461.1 109.1 %gather_fusion = f32[32768,128]{1,0:T(8,128)} fusion(f32[512,128]{1,0:T(8,128)S(1)} %bitcast.73, s32[32768]{0:T(1024)S(1)} %broadcast_clamp_fusion), kind=kCustom, calls=%fused_computation | custom fusion | bytes 33685504 | tf_op jit(solution)/shard_map/gather | solution.py:133
  570.2 11.8 select_reduce_fusion.1
  582.0 17.8 %all_to_all.30 = f32[128,2,128]{2,1,0:T(2,128)S(1)} all-to-all(f32[128,2,128]{2,1,0:T(2,128)S(1)} %bitcast.95), channel_id=1, replica_groups=mesh['lat'=8,'lon'=16] {'lat','lon'}, dimensions={0} | all-to-all | bytes 262144 | tf_op jit(solution)/shard_map/all_to_all | solution.py:135
  600.1 15.4 fusion.462
  615.7 14.2 all_to_all.31
  629.9 195.0 %scatter_custom_fusion.1 = f32[512,128]{1,0:T(8,128)S(1)} fusion(s32[32768]{0:T(1024)S(1)} %bitcast.99, f32[32768]{0:T(1024)S(1)} %bitcast.107, f32[]{:T(128)} %constant.36.clone.1, s32[32768]{0:T(1024)S(1)} %add_select_fusion), kind=kCustom, calls=%fused_computation.8 | custom fusion | flops 12582912 | bytes 525312 | tf_op jit(solution)/shard_map/scatter-add | solution.py:120
  825.3 28.9 %collective-permute-start.45 = (f32[4,1,128]{2,0,1:T(4,128)S(1)}, f32[4,1,128]{2,0,1:T(4,128)S(1)}, u32[]{:S(2)}, u32[]{:S(2)}) collective-permute-start(f32[4,1,128]{2,0,1:T(4,128)S(1)} %get-tuple-element.123), channel_id=1, source_target_pairs={{16,0},{32,16},{48,32},{64,48},{80,64},{96,80},{112,96},{0,112},{1... | collective-permute-start | bytes 6152 | tf_op jit(solution)/shard_map/ppermute | solution.py:19
  861.2 5.4 collective-permute-done.47
  935.3 67.5 %all-reduce = (f32[]{:T(128)}, f32[]{:T(128)}) all-reduce(f32[]{:T(128)} %get-tuple-element.11, f32[]{:T(128)} %get-tuple-element.10), channel_id=1, replica_groups=mesh['lat'=8,'lon'=16] {'lat','lon'}, use_global_device_ids=true, to_apply=%region_3.4 | all-reduce | flops 2 | bytes 16 | tf_op jit(solution)/shard_map/psum | solution.py:73
  1004.9 62.5 %psum.30 = f32[]{:T(128)} all-reduce(f32[]{:T(128)} %multiply_reduce_fusion.1), channel_id=1, replica_groups=mesh['lat'=8,'lon'=16] {'lat','lon'}, use_global_device_ids=true, to_apply=%region_9.10 | all-reduce | flops 1 | bytes 8 | tf_op jit(solution)/shard_map/psum | solution.py:73
  1078.2 5.2 collective-permute-done.67
  1151.6 109.1 %gather_fusion.1 = f32[32768,128]{1,0:T(8,128)} fusion(f32[512,128]{1,0:T(8,128)S(1)} %bitcast.72, s32[32768]{0:T(1024)S(1)} %broadcast_clamp_fusion), kind=kCustom, calls=%fused_computation.1 | custom fusion | bytes 33685504 | tf_op jit(solution)/shard_map/gather | solution.py:133
  1260.7 11.8 select_reduce_fusion
  1272.5 18.2 %all_to_all.32 = f32[128,2,128]{2,1,0:T(2,128)S(1)} all-to-all(f32[128,2,128]{2,1,0:T(2,128)S(1)} %bitcast.96), channel_id=1, replica_groups=mesh['lat'=8,'lon'=16] {'lat','lon'}, dimensions={0} | all-to-all | bytes 262144 | tf_op jit(solution)/shard_map/all_to_all | solution.py:135
  1291.0 15.4 fusion.463
  1306.6 14.2 all_to_all.33
  1320.8 195.0 %scatter_custom_fusion.2 = f32[512,128]{1,0:T(8,128)S(1)} fusion(s32[32768]{0:T(1024)S(1)} %bitcast.100, f32[32768]{0:T(1024)S(1)} %bitcast.106, f32[]{:T(128)} %constant.36.clone.1, s32[32768]{0:T(1024)S(1)} %add_select_fusion), kind=kCustom, calls=%fused_computation.5 | custom fusion | flops 12582912 | bytes 525312 | tf_op jit(solution)/shard_map/scatter-add | solution.py:120
  1516.1 28.9 %collective-permute-start.85 = (f32[4,1,128]{2,0,1:T(4,128)S(1)}, f32[4,1,128]{2,0,1:T(4,128)S(1)}, u32[]{:S(2)}, u32[]{:S(2)}) collective-permute-start(f32[4,1,128]{2,0,1:T(4,128)S(1)} %get-tuple-element.103), channel_id=1, source_target_pairs={{16,0},{32,16},{48,32},{64,48},{80,64},{96,80},{112,96},{0,112},{1... | collective-permute-start | bytes 6152 | tf_op jit(solution)/shard_map/ppermute | solution.py:19
  1552.0 5.2 collective-permute-done.87
  1574.3 5.0 collective-permute-start.93
  1591.4 5.0 collective-permute-start.97
  1626.2 67.4 %psum.31 = f32[]{:T(128)} all-reduce(f32[]{:T(128)} %get-tuple-element.14), channel_id=1, replica_groups=mesh['lat'=8,'lon'=16] {'lat','lon'}, use_global_device_ids=true, to_apply=%region_13.14 | all-reduce | flops 1 | bytes 8 | tf_op jit(solution)/shard_map/psum | solution.py:149
  1704.4 5.2 collective-permute-done.107
  (404 shorter events, 475.1 us)
Async XLA Ops:
  3.9 50.7 %all-to-all-start = ((s32[128,2,128]{2,1,0:T(2,128)}), s32[128,2,128]{2,1,0:T(2,128)S(1)}, u32[]{:S(2)}, u32[]{:S(2)}) async-start(s32[128,2,128]{2,1,0:T(2,128)} %bitcast.1), calls=%async_computation | async-start | bytes 262144 | tf_op jit(solution)/shard_map/all_to_all | solution.py:96
  18.9 18.0 %collective-permute-start = (f32[3,4,5,128]{3,1,2,0:T(4,128)S(1)}, f32[3,4,5,128]{3,1,2,0:T(4,128)S(1)}, u32[]{:S(2)}, u32[]{:S(2)}) collective-permute-start(f32[3,4,5,128]{3,1,2,0:T(4,128)S(1)} %get-tuple-element.21), channel_id=1, source_target_pairs={{0,16},{16,32},{32,48},{48,64},{64,80},{80,96},{96,112},{112,0},{1... | collective-permute-start | bytes 92168 | tf_op jit(solution)/shard_map/ppermute | solution.py:16
  20.6 16.2 collective-permute-start.1
  38.6 11.8 collective-permute-start.3
  54.7 17.3 all-to-all-start.1
  267.3 30.2 %collective-permute-start.5 = (f32[4,1,128]{2,0,1:T(4,128)S(1)}, f32[4,1,128]{2,0,1:T(4,128)S(1)}, u32[]{:S(2)}, u32[]{:S(2)}) collective-permute-start(f32[4,1,128]{2,0,1:T(4,128)S(1)} %get-tuple-element.143), channel_id=1, source_target_pairs={{16,0},{32,16},{48,32},{64,48},{80,64},{96,80},{112,96},{0,112},{1... | collective-permute-start | bytes 6152 | tf_op jit(solution)/shard_map/ppermute | solution.py:19
  299.9 8.6 collective-permute-start.7
  315.6 8.6 collective-permute-start.11
  332.9 8.6 collective-permute-start.15
  350.2 9.1 collective-permute-start.19
  367.4 8.7 collective-permute-start.23
  384.1 8.7 collective-permute-start.27
  400.9 8.7 collective-permute-start.31
  417.7 8.7 collective-permute-start.35
  434.5 8.7 collective-permute-start.39
  451.2 8.8 collective-permute-start.43
  825.3 30.3 %collective-permute-start.45 = (f32[4,1,128]{2,0,1:T(4,128)S(1)}, f32[4,1,128]{2,0,1:T(4,128)S(1)}, u32[]{:S(2)}, u32[]{:S(2)}) collective-permute-start(f32[4,1,128]{2,0,1:T(4,128)S(1)} %get-tuple-element.123), channel_id=1, source_target_pairs={{16,0},{32,16},{48,32},{64,48},{80,64},{96,80},{112,96},{0,112},{1... | collective-permute-start | bytes 6152 | tf_op jit(solution)/shard_map/ppermute | solution.py:19
  857.8 8.8 collective-permute-start.47
  908.3 8.7 collective-permute-start.59
  925.0 8.7 collective-permute-start.63
  1108.3 8.7 collective-permute-start.75
  1125.1 8.7 collective-permute-start.79
  1141.9 8.7 collective-permute-start.83
  1516.1 30.3 %collective-permute-start.85 = (f32[4,1,128]{2,0,1:T(4,128)S(1)}, f32[4,1,128]{2,0,1:T(4,128)S(1)}, u32[]{:S(2)}, u32[]{:S(2)}) collective-permute-start(f32[4,1,128]{2,0,1:T(4,128)S(1)} %get-tuple-element.103), channel_id=1, source_target_pairs={{16,0},{32,16},{48,32},{64,48},{80,64},{96,80},{112,96},{0,112},{1... | collective-permute-start | bytes 6152 | tf_op jit(solution)/shard_map/ppermute | solution.py:19
  1564.5 8.8 collective-permute-start.91
  1599.1 8.7 collective-permute-start.99
  1615.9 8.7 collective-permute-start.103
  1700.7 9.0 collective-permute-start.107
  1716.2 8.8 collective-permute-start.111
  1733.6 8.7 collective-permute-start.115
  1750.6 8.7 collective-permute-start.119
  1767.4 8.7 collective-permute-start.123
  (99 other events, 1304.9 us)
where the time goes:
time: 1790 us; the launch traced here: 1780 us
  other arithmetic  651 us (36%)
  waiting for transfers between devices  296 us (17%)
  starting transfers between devices  283 us (16%)
  blocking collectives  262 us (15%)
  local copies, waits for them, and re-layouts  231 us (13%)
  matrix products  49.7 us (3%)
    scatter-add x3, other arithmetic, adjoint(): jnp.zeros((tile_lines, tile_cols), jnp.float32).at[line_index].add(spread)  585 us
    ppermute x62, starting transfers between devices, with_halo(): lax.ppermute(lax.slice_in_dim(block, 0, width, axis=dim), axis, backward)  223 us
    gather x2, local copies, waits for them, and re-layouts, body(): lines = hessian_field.reshape(tile_lines, tile_cols)[line_index]  218 us
    ppermute x62, waiting for transfers between devices, with_halo(): lax.ppermute(lax.slice_in_dim(block, block.shape[dim] - width, None, axis...  148 us
    ppermute x62, waiting for transfers between devices, with_halo(): lax.ppermute(lax.slice_in_dim(block, 0, width, axis=dim), axis, backward)  138 us
    psum x2, blocking collectives, squares(): return lax.psum(jnp.sum(residual * residual), ('lat', 'lon'))  130 us
    psum x1, blocking collectives, body(): alpha = norm_now / lax.psum(jnp.sum(direction * image), ('lat', 'lon'))  67.4 us
    dot_general x3, matrix products, weigh(): jnp.einsum('kij,kj->ki', obs_weights, values, precision=lax.Precision.HIG...  46.1 us
  transfers between devices with their start and end apart: 126, of which 118 were waited for; matrix products, arithmetic and copies ran while one was open for 2% of the time, Pallas kernels for 0%

commit v1 on v0

v1 whole, which is shorter than its diff:
```python
import functools

import jax
import jax.numpy as jnp
from jax import lax
from jax.experimental import pallas as pl
from jax.experimental.pallas import tpu as pltpu
from jax.sharding import PartitionSpec as P

PASSES = 5
EDGE = 16
GROUP = 8
STEP = 16
MESH = pl.DeviceIdType.MESH
EXACT = lax.Precision.HIGHEST
VMEM = pl.BlockSpec(memory_space=pltpu.VMEM)


def split(value):
    high = value.astype(jnp.bfloat16)
    low = (value - high.astype(jnp.float32)).astype(jnp.bfloat16)
    return high, low


def places(cells):
    line = cells >> 7
    return line & 255, ((line >> 8) << 7) + (cells & 127)


def hits(numbers, width):
    lines = lax.broadcasted_iota(jnp.int32, (256, width), 0)
    return lines == numbers


def neighbours():
    lats, lons = lax.axis_size("lat"), lax.axis_size("lon")
    lat, lon = lax.axis_index("lat"), lax.axis_index("lon")
    steps = [(1, 0), (-1, 0), (0, 1), (0, -1), (1, 1), (1, -1), (-1, 1), (-1, -1)]
    return [(lax.rem(lat + a + lats, lats), lax.rem(lon + b + lons, lons)) for a, b in steps]


def greet_neighbours():
    partners = neighbours()
    barrier = pltpu.get_barrier_semaphore()
    for partner in partners:
        pl.semaphore_signal(barrier, inc=1, device_id=partner, device_id_type=MESH)
    pl.semaphore_wait(barrier, len(partners))


def swap_edges(field_ref, low_ref, high_ref, edges, send, receive):
    partners = neighbours()
    rows = field_ref.shape[1]
    top = field_ref.at[:, rows - EDGE : rows, :]
    bottom = field_ref.at[:, 0:EDGE, :]
    sources = [top, bottom, high_ref, low_ref, top, top, bottom, bottom]
    landing = [1, 0, 3, 2, 7, 6, 5, 4]
    copies = []
    for number in (0, 1, 4, 5, 6, 7, 2, 3):
        partner = partners[number]
        copy = pltpu.make_async_remote_copy(
            src_ref=sources[number],
            dst_ref=edges.at[landing[number]],
            send_sem=send.at[number],
            recv_sem=receive.at[landing[number]],
            device_id=partner,
            device_id_type=MESH,
        )
        copy.start()
        copies.append(copy)
    return copies


def assemble(level, field_ref, edges):
    shape = (EDGE, field_ref.shape[2])
    lane = lax.broadcasted_iota(jnp.int32, shape, 1)

    def corner(east, west):
        inner = jnp.where(lane >= shape[1] - EDGE, edges[west, level], 0.0)
        return jnp.where(lane < EDGE, edges[east, level], inner)

    gap = jnp.zeros((shape[1] - 2 * EDGE, field_ref.shape[1]), jnp.float32)
    beside = jnp.concatenate([edges[2, level], gap, edges[3, level]], 0).T
    upper = jnp.concatenate([field_ref[level], beside], 1)
    north = jnp.concatenate([edges[0, level], corner(4, 5)], 1)
    south = jnp.concatenate([edges[1, level], corner(6, 7)], 1)
    return jnp.concatenate([upper, north, south], 0)


def faces_kernel(field_ref, low_ref, high_ref, out_ref, edges, send, receive):
    greet_neighbours()
    for copy in swap_edges(field_ref, low_ref, high_ref, edges, send, receive):
        copy.wait()
    levels = out_ref.shape[1]
    rows, columns = out_ref.shape[2:]
    tile_rows = field_ref.shape[1]
    line = lax.broadcasted_iota(jnp.int32, (rows, columns), 0)
    line = jnp.where(line < tile_rows + EDGE, line, line - tile_rows - 2 * EDGE)
    line = lax.axis_index("lat") * tile_rows + line
    inside = (line >= 0) & (line < tile_rows * lax.axis_size("lat"))

    def per_level(level, carry):
        land = jnp.where(inside, assemble(level, field_ref, edges), 0.0)
        east = assemble(levels + level, field_ref, edges)
        north = assemble(2 * levels + level, field_ref, edges)
        east = east * land * pltpu.roll(land, columns - 1, 1)
        north = north * land * pltpu.roll(land, rows - 1, 0)
        out_ref[0, level] = east
        out_ref[1, level] = pltpu.roll(east, 1, 1)
        out_ref[2, level] = north
        out_ref[3, level] = pltpu.roll(north, 1, 0)
        return carry

    lax.fori_loop(0, levels, per_level, 0)


def edge_scratch(levels, columns):
    return [
        pltpu.VMEM((8, levels, EDGE, columns), jnp.float32),
        pltpu.SemaphoreType.DMA((8,)),
        pltpu.SemaphoreType.DMA((8,)),
    ]


def faces(stacked):
    levels, rows, columns = stacked.shape
    low = jnp.swapaxes(stacked[:, :, :EDGE], 1, 2)
    high = jnp.swapaxes(stacked[:, :, columns - EDGE :], 1, 2)
    return pl.pallas_call(
        faces_kernel,
        out_shape=jax.ShapeDtypeStruct((4, levels // 3, rows + 2 * EDGE, 2 * columns), jnp.float32),
        in_specs=[VMEM] * 3,
        out_specs=VMEM,
        scratch_shapes=edge_scratch(levels, columns),
        compiler_params=remote(0),
        name="faces",
    )(stacked, low, high)


def remote(number):
    return pltpu.CompilerParams(
        vmem_limit_bytes=48 * 1024 * 1024, collective_id=number, has_side_effects=True
    )


def everyone():
    lats, lons = lax.axis_size("lat"), lax.axis_size("lon")
    return lats * lons, lax.axis_index("lat") * lons + lax.axis_index("lon")


def where_is(device):
    lons = lax.axis_size("lon")
    return lax.div(device, lons), lax.rem(device, lons)


def greet_everyone():
    devices, me = everyone()
    barrier = pltpu.get_barrier_semaphore()

    def greet(distance, carry):
        partner = where_is(lax.rem(me + distance, devices))
        pl.semaphore_signal(barrier, inc=1, device_id=partner, device_id_type=MESH)
        return carry

    lax.fori_loop(1, devices, greet, 0)
    pl.semaphore_wait(barrier, devices - 1)


def push(source, target, send, receive, device):
    pltpu.make_async_remote_copy(
        src_ref=source,
        dst_ref=target,
        send_sem=send,
        recv_sem=receive,
        device_id=where_is(device),
        device_id_type=MESH,
    ).start()


def wait_for(ref, semaphore):
    pltpu.make_async_copy(ref, ref, semaphore).wait()


def gather_and_send(here, field_ref, turned, found_ref, back, send, receive):
    square = jnp.concatenate([field_ref[0:256], field_ref[256:512]], 1).T
    high, low = split(square)
    turned[0:256] = high
    turned[256:512] = low
    devices, me = everyone()
    ranks, width = here.shape[1:]
    batch = GROUP // ranks
    groups = devices // batch

    def group_of(turn):
        return lax.rem(lax.div(me, batch) + turn, groups)

    def send_group(turn):
        for item in range(batch):
            device = group_of(turn) * batch + item

            @pl.when(device != me)
            def _():
                push(found_ref.at[device], back.at[me], send, receive, device)

            @pl.when(device == me)
            def _():
                pltpu.make_async_copy(found_ref.at[device], back.at[device], receive).start()

    def step(turn, carry):
        start = group_of(turn) * batch
        places_of = [
            places(here[start + item // ranks, item % ranks : item % ranks + 1])
            for item in range(GROUP)
        ]
        right = [
            jnp.where(hits(row, width), 1.0, 0.0).astype(jnp.bfloat16) for row, _ in places_of
        ]
        found = jnp.dot(
            turned[...], jnp.concatenate(right, 1), preferred_element_type=jnp.float32
        )
        found = found[0:256] + found[256:512]
        for item in range(GROUP):
            part = found[:, item * width : (item + 1) * width]
            part = jnp.where(hits(places_of[item][1], width), part, 0.0)
            spot = item % ranks
            found_ref[start + item // ranks, spot : spot + 1] = jnp.sum(part, 0, keepdims=True)

        @pl.when(turn > 0)
        def _():
            send_group(turn - 1)

        return carry

    lax.fori_loop(0, groups, step, 0)
    send_group(groups - 1)
    wait_for(back, receive)


def weigh(turned, weights_ref, weighted):
    held = turned.shape[1]

    def step(number, carry):
        values = turned[...]
        start = pl.multiple_of(number * STEP, STEP)
        rows = []
        for item in range(STEP):
            column = values[:, item : item + 1]
            rows.append(jnp.sum(weights_ref[start + item] * column, 0, keepdims=True))
        weighted[pl.ds(start, STEP), :] = jnp.concatenate(rows, 0)
        turned[...] = pltpu.roll(values, held - STEP, 1)
        return carry

    lax.fori_loop(0, held // STEP, step, 0)


def scatter_arrivals(first, here, parcel, arrived, total, send, receive):
    devices, me = everyone()
    ranks, width = here.shape[1:]
    batch = GROUP // ranks
    groups = devices // batch
    mine = lax.div(me, batch)

    pltpu.make_async_copy(parcel.at[me], arrived.at[me], receive.at[mine]).start()

    def tell(distance, carry):
        device = lax.rem(me + distance, devices)
        push(parcel.at[device], arrived.at[me], send, receive.at[mine], device)
        return carry

    lax.fori_loop(1, devices, tell, 0)

    def step(turn, carry):
        group = lax.rem(mine + 2 * groups - 1 - turn, groups)
        start = group * batch
        wait_for(arrived.at[pl.ds(start, batch)], receive.at[group])
        left, right = [], []
        for item in range(GROUP):
            device, spot = start + item // ranks, item % ranks
            if first:
                cells = arrived[device, spot : spot + 1].astype(jnp.int32)
                here[device, spot : spot + 1] = cells
                value = arrived[device, ranks + spot : ranks + spot + 1]
            else:
                cells = here[device, spot : spot + 1]
                value = arrived[device, spot : spot + 1]
            row, column = places(cells)
            high = value.astype(jnp.bfloat16).astype(jnp.float32)
            row_hit = hits(row, width)
            spread = [jnp.where(row_hit, part, 0.0) for part in (high, value - high)]
            left.append(jnp.concatenate(spread, 0).astype(jnp.bfloat16))
            right.append(jnp.where(hits(column, width), 1.0, 0.0).astype(jnp.bfloat16))
        total[...] += lax.dot_general(
            jnp.concatenate(left, 1),
            jnp.concatenate(right, 1),
            (((1,), (1,)), ((), ())),
            preferred_element_type=jnp.float32,
        )
        return carry

    lax.fori_loop(0, groups, step, 0)


def phase_kernel(mode, *refs):
    first, last = mode == "first", mode == "last"
    place_ref, weights_hbm, faces_ref, sigma_ref = refs[:4]
    refs = refs[4:]
    if first:
        cells_ref, value_ref, smoothed, field_out, here = refs[:5]
        refs = refs[5:]
    elif last:
        here, seen_ref, base_ref, once_ref, smoothed, scale_out = refs[:6]
        refs = refs[6:]
    else:
        here, seen_ref, smoothed, field_out = refs[:4]
        refs = refs[4:]
    weights_ref, turned, weighted, parcel, arrived, total, field_ref, low, high, work = refs[:10]
    copied, send, receive, edges, edge_send, edge_receive = refs[10:16]
    refs = refs[16:]
    if not first:
        square, found, back, found_send, found_receive = refs[:5]
        refs = refs[5:]
    if last:
        part, parts, part_send, part_receive = refs

    load = pltpu.make_async_copy(weights_hbm, weights_ref, copied)
    load.start()
    greet_everyone()
    devices, me = everyone()
    ranks, width = here.shape[1:]
    held = turned.shape[1]
    number = lax.broadcasted_iota(jnp.int32, (devices, held), 0)

    def placing(rank):
        return jnp.where(number * ranks + rank == place_ref[0:1], 1.0, 0.0)

    if first:
        turned[...] = value_ref[...].T
    else:
        gather_and_send(here, seen_ref, square, found, back, found_send, found_receive)
        turned[...] = sum(
            lax.dot_general(
                back[:, rank, :],
                placing(rank),
                (((0,), (0,)), ((), ())),
                precision=EXACT,
                preferred_element_type=jnp.float32,
            )
            for rank in range(ranks)
        )
    load.wait()
    weigh(turned, weights_ref, weighted)
    for rank in range(ranks):
        chosen = placing(rank)
        if first:
            parcel[:, rank, :] = jnp.dot(
                chosen,
                cells_ref[...].astype(jnp.float32),
                precision=EXACT,
                preferred_element_type=jnp.float32,
            )
        parcel[:, (ranks if first else 0) + rank, :] = jnp.dot(
            chosen, weighted[...], precision=EXACT, preferred_element_type=jnp.float32
        )
    total[...] = jnp.zeros_like(total)
    scatter_arrivals(first, here, parcel, arrived, total, send, receive)

    field = total[0:256] + total[256:512]
    levels, tile_rows, tile_columns = field_ref.shape
    for level in range(levels):
        start, side = level * 128 % 256, level * 128 // 256 * 128
        tile = field[start : start + 128, side : side + 128] * sigma_ref[level]
        field_ref[level] = tile
        flat = tile.T
        low[level] = flat[0:EDGE]
        high[level] = flat[tile_columns - EDGE :]
    copies = swap_edges(field_ref, low, high, edges, edge_send, edge_receive)
    for copy in copies:
        copy.wait()
    rows, columns = work.shape[1:]

    def one_pass(level, x):
        result = x + faces_ref[0, level] * (pltpu.roll(x, columns - 1, 1) - x)
        result += faces_ref[1, level] * (pltpu.roll(x, 1, 1) - x)
        result += faces_ref[2, level] * (pltpu.roll(x, rows - 1, 0) - x)
        result += faces_ref[3, level] * (pltpu.roll(x, 1, 0) - x)
        work[level] = result

    def per_level(level, carry):
        one_pass(level, assemble(level, field_ref, edges))
        for sweep in range(PASSES - 1):
            one_pass(level, work[level])
        tile = work[level, 0:tile_rows, 0:tile_columns]
        smoothed[level] = tile
        if not last:
            for sweep in range(PASSES):
                one_pass(level, work[level])
            tile = work[level, 0:tile_rows, 0:tile_columns]
            start = pl.multiple_of(level * tile_rows, tile_rows)
            field_out[pl.ds(start, tile_rows), :] = sigma_ref[level] * tile
            return carry
        base, once = base_ref[level], once_ref[level]
        products = (base * base, base * once, once * once, once * tile)
        return tuple(c + jnp.sum(p, 0, keepdims=True) for c, p in zip(carry, products))

    sums = tuple(jnp.zeros((1, tile_columns), jnp.float32) for _ in range(4))
    sums = lax.fori_loop(0, levels, per_level, sums)
    if last:
        lane = lax.broadcasted_iota(jnp.int32, (1, tile_columns), 1)
        row = jnp.zeros((1, tile_columns), jnp.float32)
        for spot in range(4):
            row = jnp.where(lane == spot, jnp.sum(sums[spot], 1, keepdims=True), row)
        part[...] = row
        wait_for(arrived.at[pl.ds(0, devices - 1)], send)
        wait_for(back.at[pl.ds(0, devices - 1)], found_send)

        def tell(distance, carry):
            device = lax.rem(me + distance, devices)
            push(part, parts.at[distance - 1], part_send, part_receive, device)
            return carry

        lax.fori_loop(1, devices, tell, 0)
        wait_for(parts, part_receive)
        row = row + jnp.sum(parts[...], 0)
        s0, s1, s2, s3 = (
            jnp.sum(jnp.where(lane == spot, row, 0.0), 1, keepdims=True) for spot in range(4)
        )
        alpha = s0 / (s0 + s1)
        rest = s1 / (s0 + s1)
        norm = alpha * (alpha * s2 - rest * s1)
        along = rest + norm / s0
        norm_next = along * along * s0 - 2 * along * alpha * s1 + alpha * alpha * s2
        energy = along * along * s1 - 2 * along * alpha * s2 + alpha * alpha * s3
        step = norm / (norm_next + energy)
        scales = [
            alpha + step * along,
            step * alpha,
            rest - step * along,
            step * alpha - alpha - step * along,
        ]
        for spot in range(4):
            row = jnp.where(lane == spot, scales[spot], row)
        scale_out[...] = row
        wait_for(parts, part_send)
    else:
        wait_for(arrived.at[pl.ds(0, devices - 1)], send)
        if not first:
            wait_for(back.at[pl.ds(0, devices - 1)], found_send)


def phase(mode, number, place, obs_weights, weights, sigma, *more):
    first, last = mode == "first", mode == "last"
    held, width = obs_weights.shape[:2]
    devices = lax.axis_size("lat") * lax.axis_size("lon")
    levels, rows, columns = sigma.shape
    real = jnp.float32
    tile = jax.ShapeDtypeStruct(sigma.shape, real)
    flat = jax.ShapeDtypeStruct((levels * rows, columns), real)
    if first:
        outs = (tile, flat, jax.ShapeDtypeStruct((devices, 2, width), jnp.int32))
    elif last:
        outs = (tile, jax.ShapeDtypeStruct((1, columns), real))
    else:
        outs = (tile, flat)
    parcel = pltpu.VMEM((devices, 4 if first else 2, width), real)
    dma = pltpu.SemaphoreType.DMA
    scratch = [
        pltpu.VMEM(obs_weights.shape, real),
        pltpu.VMEM((width, held), real),
        pltpu.VMEM((held, width), real),
        parcel,
        parcel,
        pltpu.VMEM((512, 256), real),
        pltpu.VMEM(sigma.shape, real),
        pltpu.VMEM((levels, EDGE, rows), real),
        pltpu.VMEM((levels, EDGE, rows), real),
        pltpu.VMEM(weights.shape[1:], real),
        dma,
        dma,
        dma((devices * 2 // GROUP,)),
    ] + edge_scratch(levels, columns)
    if not first:
        scratch += [pltpu.VMEM((512, 256), jnp.bfloat16), parcel, parcel, dma, dma]
    if last:
        scratch += [
            pltpu.VMEM((1, columns), real),
            pltpu.VMEM((devices - 1, 1, columns), real),
            dma,
            dma,
        ]
    inputs = (place, obs_weights, weights, sigma) + more
    specs = [VMEM] * len(inputs)
    specs[1] = pl.BlockSpec(memory_space=pl.ANY)
    return pl.pallas_call(
        functools.partial(phase_kernel, mode),
        out_shape=outs,
        in_specs=specs,
        out_specs=(VMEM,) * len(outs),
        scratch_shapes=scratch,
        compiler_params=remote(number),
        name=mode,
    )(*inputs)


def body(sigma, east_coef, north_coef, mask, innovations, cells, owner, obs_weights):
    held = cells.shape[0]
    target = owner[:, 0]
    order = jnp.arange(held, dtype=jnp.int32)
    before = (target[:, None] == target[None, :]) & (order[:, None] < order[None, :])
    rank = jnp.sum(before.astype(jnp.int32), axis=0)
    place = jnp.stack([target * 2 + rank] * 8)
    stacked = jnp.concatenate([mask.astype(jnp.float32), east_coef, north_coef])
    weights = faces(stacked)
    fixed = (place, obs_weights, weights, sigma)
    base, base_field, here = phase("first", 1, *fixed, cells, innovations)
    once, once_field = phase("middle", 2, *fixed, here, base_field)
    again, scale = phase("last", 3, *fixed, here, once_field, base, once)
    scale = scale[0]
    increment = (scale[0] * base_field - scale[1] * once_field).reshape(sigma.shape)
    residual = scale[2] * base + scale[3] * once + scale[1] * again
    return (increment, residual)


def solution(mesh):
    return jax.shard_map(
        body,
        mesh=mesh,
        in_specs=(
            P(None, "lat", "lon"),
            P(None, "lat", "lon"),
            P(None, "lat", "lon"),
            P(None, "lat", "lon"),
            P(("lat", "lon"), None),
            P(("lat", "lon"), None),
            P(("lat", "lon"), None),
            P(("lat", "lon"), None, None),
        ),
        out_specs=(P(None, "lat", "lon"), P(None, "lat", "lon")),
        check_vma=False,
    )
```

time: 1790 us -> 205 us (0.11)
  other arithmetic: 651 us -> 6.2 us
  waiting for transfers between devices: 296 us -> 0 us
  starting transfers between devices: 283 us -> 0 us
  blocking collectives: 262 us -> 0 us
  local copies, waits for them, and re-layouts: 231 us -> 4.2 us
  Pallas kernels: 0 us -> 193 us
  matrix products: 49.7 us -> 0 us
    scatter-add x3 -> x0, other arithmetic: 585 us -> none  [adjoint(): jnp.zeros((tile_lines, tile_cols), jnp.float32).at[line_index].add(spread)]
    ppermute x124 -> x0, waiting for transfers between devices: 286 us -> none  [the longest x62 148 us: with_halo(): lax.ppermute(lax.slice_in_dim(block, block.shape[dim] - width, None, axis...]
    ppermute x124 -> x0, starting transfers between devices: 264 us -> none  [the longest x62 223 us: with_halo(): lax.ppermute(lax.slice_in_dim(block, 0, width, axis=dim), axis, backward)]
    gather x2 -> x0, local copies, waits for them, and re-layouts: 218 us -> none  [body(): lines = hessian_field.reshape(tile_lines, tile_cols)[line_index]]
    psum x3 -> x0, blocking collectives: 197 us -> none  [the longest x2 130 us: squares(): return lax.psum(jnp.sum(residual * residual), ('lat', 'lon'))]
    pallas_call x0 -> x4, Pallas kernels: none -> 193 us  [the longest x3 178 us: phase(): pl.pallas_call(functools.partial(phase_kernel, mode), out_shape=outs, in_...]
    all_to_all x4 -> x0, blocking collectives: 64.4 us -> none  [the longest x2 36 us: body(): lax.all_to_all(observe_values.reshape(devices, capacity, block_width), ('...]
    dot_general x9 -> x0, matrix products: 49.7 us -> none  [the longest x3 46.1 us: weigh(): jnp.einsum('kij,kj->ki', obs_weights, values, precision=lax.Precision.HIG...]
  transfers between devices with their start and end apart: 126 -> 0, of which waited for: 118 -> 0; matrix products, arithmetic and copies ran while one was open for 2% -> 0% of each run, Pallas kernels for 0% -> 0%
where the time goes in v1:
time: 205 us; the launch traced here: 204 us
  Pallas kernels  193 us (94%)
  other arithmetic  6.2 us (3%)
  local copies, waits for them, and re-layouts  4.2 us (2%)
    pallas_call x3, Pallas kernels, phase(): pl.pallas_call(functools.partial(phase_kernel, mode), out_shape=outs, in_...  178 us
    pallas_call x1, Pallas kernels, faces(): pl.pallas_call(faces_kernel, out_shape=jax.ShapeDtypeStruct((4, levels //...  14.8 us

profile of v1, /device:TPU:1, one launch (start us, length us, event | category | flops | bytes accessed | tf_op | source)
XLA Modules:
  0.0 204.3 jit_solution(28518360718031870)
XLA Ops:
  0.6 0.0 copy-start
  0.6 0.0 copy-start.1
  0.6 0.0 copy-start.2
  0.7 0.8 convert_reduce_fusion
  1.5 0.7 multiply_add_fusion.1
  2.2 1.1 copy.15
  3.2 1.1 copy.16
  4.3 1.1 copy.14
  5.4 0.1 pad_maximum_fusion
  5.5 0.3 copy.17.field_ref
  5.8 14.8 %faces.1.refs_2_ = f32[4,4,160,256]{3,2,1,0:T(8,128)S(1)} custom-call(f32[12,128,128]{2,1,0:T(8,128)S(1)} %copy.17.field_ref, f32[12,16,128]{2,1,0:T(8,128)S(1)} %get-tuple-element.17.low_ref, f32[12,16,128]{2,1,0:T(8,128)S(1)} %get-tuple-element.16.high_ref), custom_call_target="tpu_custom_call" | custom-call | tf_op jit(solution)/shard_map/faces/pallas_call | solution.py:128
  20.7 0.0 copy-done
  20.7 0.0 copy-done.1
  20.7 0.0 copy-done.2
  20.7 47.3 %first.1 = (f32[4,128,128]{2,1,0:T(8,128)S(1)}, f32[512,128]{1,0:T(8,128)S(1)}, s32[128,2,128]{2,1,0:T(2,128)S(1)}) custom-call(s32[8,128]{1,0:T(8,128)S(1)} %stack.2.refs_0_, f32[128,128,128]{2,1,0:T(8,128)} %refs_1_.5, f32[4,4,160,256]{3,2,1,0:T(8,128)S(1)} %faces.1.refs_2_, f32[4,128,128]{2,1,0:T(8,128)S(1)} %copy-done, s32[128,128]{1,0:T(8,128)S(1)} %copy-done.1, ...), custom_call_target="tpu_custom_call" | custom-call | tf_op jit(solution)/shard_map/first/pallas_call | solution.py:492
  68.0 63.2 %middle.1 = (f32[4,128,128]{2,1,0:T(8,128)S(1)}, f32[512,128]{1,0:T(8,128)S(1)}) custom-call(s32[8,128]{1,0:T(8,128)S(1)} %stack.2.refs_0_, f32[128,128,128]{2,1,0:T(8,128)} %refs_1_.5, f32[4,4,160,256]{3,2,1,0:T(8,128)S(1)} %faces.1.refs_2_, f32[4,128,128]{2,1,0:T(8,128)S(1)} %copy-done, s32[128,2,128]{2,1,0:T(2,128)S(1)} %get-tuple-element.9.refs_4_, ...), custom_call_target="tpu_custom_call" | custom-call | tf_op jit(solution)/shard_map/middle/pallas_call | solution.py:492
  131.2 67.7 %last.1 = (f32[4,128,128]{2,1,0:T(8,128)S(1)}, f32[1,128]{1,0:T(1,128)S(1)}) custom-call(s32[8,128]{1,0:T(8,128)S(1)} %stack.2.refs_0_, f32[128,128,128]{2,1,0:T(8,128)} %refs_1_.5, f32[4,4,160,256]{3,2,1,0:T(8,128)S(1)} %faces.1.refs_2_, f32[4,128,128]{2,1,0:T(8,128)S(1)} %copy-done, s32[128,2,128]{2,1,0:T(2,128)S(1)} %get-tuple-element.9.refs_4_, ...), custom_call_target="tpu_custom_call" | custom-call | tf_op jit(solution)/shard_map/last/pallas_call | solution.py:492
  199.0 0.7 fusion.1
  199.7 2.6 %multiply_add_fusion = f32[4,128,128]{2,1,0:T(8,128)} fusion(f32[4,128,128]{2,1,0:T(8,128)S(1)} %get-tuple-element.15, f32[4,128,128]{2,1,0:T(8,128)S(1)} %get-tuple-element.13.refs_7_, f32[4,128,128]{2,1,0:T(8,128)S(1)} %get-tuple-element.12.refs_6_, f32[]{:T(128)} %bitcast.4, f32[]{:T(128)} %bitcast.7, f32[]{:T(128)} %bitcast.6), kind=kLoop, calls=%fused_computation.1 | loop fusion | flops 327680 | bytes 1048588 | tf_op jit(solution)/shard_map/add | solution.py:518
  202.3 2.0 multiply_subtract_fusion
  (3 shorter events, 0.0 us)
Async XLA Ops:
  0.6 20.0 %copy-start = (f32[4,128,128]{2,1,0:T(8,128)S(1)}, f32[4,128,128]{2,1,0:T(8,128)}, u32[]{:S(2)}) copy-start(f32[4,128,128]{2,1,0:T(8,128)} %refs_3_.5) | copy-start | bytes 786436
  0.6 20.0 %copy-start.1 = (s32[128,128]{1,0:T(8,128)S(1)}, s32[128,128]{1,0:T(8,128)}, u32[]{:S(2)}) copy-start(s32[128,128]{1,0:T(8,128)} %refs_4_.1) | copy-start | bytes 196612
  0.6 20.0 %copy-start.2 = (f32[128,128]{1,0:T(8,128)S(1)}, f32[128,128]{1,0:T(8,128)}, u32[]{:S(2)}) copy-start(f32[128,128]{1,0:T(8,128)} %refs_5_.1) | copy-start | bytes 196612

commit v2 on v1

--- a/solution.py
+++ b/solution.py
@@ -9,7 +9,7 @@
 
 PASSES = 5
 EDGE = 16
-GROUP = 8
+GROUP = 16
 STEP = 16
 MESH = pl.DeviceIdType.MESH
 EXACT = lax.Precision.HIGHEST
@@ -24,12 +24,19 @@
 
 def places(cells):
     line = cells >> 7
-    return line & 255, ((line >> 8) << 7) + (cells & 127)
+    numbers = line & 255, ((line >> 8) << 7) + (cells & 127)
+    return numbers
 
 
 def hits(numbers, width):
     lines = lax.broadcasted_iota(jnp.int32, (256, width), 0)
     return lines == numbers
+
+
+def narrow_hits(numbers, width):
+    lines = lax.broadcasted_iota(jnp.int32, (256, width), 0)
+    narrow = [n.astype(jnp.float32).astype(jnp.bfloat16) for n in (lines, numbers)]
+    return narrow[0] == narrow[1]
 
 
 def neighbours():
@@ -37,14 +44,6 @@
     lat, lon = lax.axis_index("lat"), lax.axis_index("lon")
     steps = [(1, 0), (-1, 0), (0, 1), (0, -1), (1, 1), (1, -1), (-1, 1), (-1, -1)]
     return [(lax.rem(lat + a + lats, lats), lax.rem(lon + b + lons, lons)) for a, b in steps]
-
-
-def greet_neighbours():
-    partners = neighbours()
-    barrier = pltpu.get_barrier_semaphore()
-    for partner in partners:
-        pl.semaphore_signal(barrier, inc=1, device_id=partner, device_id_type=MESH)
-    pl.semaphore_wait(barrier, len(partners))
 
 
 def swap_edges(field_ref, low_ref, high_ref, edges, send, receive):
@@ -86,22 +85,19 @@
     return jnp.concatenate([upper, north, south], 0)
 
 
-def faces_kernel(field_ref, low_ref, high_ref, out_ref, edges, send, receive):
-    greet_neighbours()
-    for copy in swap_edges(field_ref, low_ref, high_ref, edges, send, receive):
-        copy.wait()
+def build_faces(stacked_ref, edges, out_ref):
     levels = out_ref.shape[1]
     rows, columns = out_ref.shape[2:]
-    tile_rows = field_ref.shape[1]
+    tile_rows = stacked_ref.shape[1]
     line = lax.broadcasted_iota(jnp.int32, (rows, columns), 0)
     line = jnp.where(line < tile_rows + EDGE, line, line - tile_rows - 2 * EDGE)
     line = lax.axis_index("lat") * tile_rows + line
     inside = (line >= 0) & (line < tile_rows * lax.axis_size("lat"))
 
     def per_level(level, carry):
-        land = jnp.where(inside, assemble(level, field_ref, edges), 0.0)
-        east = assemble(levels + level, field_ref, edges)
-        north = assemble(2 * levels + level, field_ref, edges)
+        land = jnp.where(inside, assemble(level, stacked_ref, edges), 0.0)
+        east = assemble(levels + level, stacked_ref, edges)
+        north = assemble(2 * levels + level, stacked_ref, edges)
         east = east * land * pltpu.roll(land, columns - 1, 1)
         north = north * land * pltpu.roll(land, rows - 1, 0)
         out_ref[0, level] = east
@@ -119,21 +115,6 @@
         pltpu.SemaphoreType.DMA((8,)),
         pltpu.SemaphoreType.DMA((8,)),
     ]
-
-
-def faces(stacked):
-    levels, rows, columns = stacked.shape
-    low = jnp.swapaxes(stacked[:, :, :EDGE], 1, 2)
-    high = jnp.swapaxes(stacked[:, :, columns - EDGE :], 1, 2)
-    return pl.pallas_call(
-        faces_kernel,
-        out_shape=jax.ShapeDtypeStruct((4, levels // 3, rows + 2 * EDGE, 2 * columns), jnp.float32),
-        in_specs=[VMEM] * 3,
-        out_specs=VMEM,
-        scratch_shapes=edge_scratch(levels, columns),
-        compiler_params=remote(0),
-        name="faces",
-    )(stacked, low, high)
 
 
 def remote(number):
@@ -189,6 +170,7 @@
     ranks, width = here.shape[1:]
     batch = GROUP // ranks
     groups = devices // batch
+    zero, one = jnp.bfloat16(0), jnp.bfloat16(1)
 
     def group_of(turn):
         return lax.rem(lax.div(me, batch) + turn, groups)
@@ -212,7 +194,7 @@
             for item in range(GROUP)
         ]
         right = [
-            jnp.where(hits(row, width), 1.0, 0.0).astype(jnp.bfloat16) for row, _ in places_of
+            jnp.where(narrow_hits(row, width), one, zero) for row, _ in places_of
         ]
         found = jnp.dot(
             turned[...], jnp.concatenate(right, 1), preferred_element_type=jnp.float32
@@ -252,12 +234,13 @@
     lax.fori_loop(0, held // STEP, step, 0)
 
 
-def scatter_arrivals(first, here, parcel, arrived, total, send, receive):
+def scatter_arrivals(first, here, parcel, arrived, total, send, receive, between):
     devices, me = everyone()
     ranks, width = here.shape[1:]
     batch = GROUP // ranks
     groups = devices // batch
     mine = lax.div(me, batch)
+    zero, one = jnp.bfloat16(0), jnp.bfloat16(1)
 
     pltpu.make_async_copy(parcel.at[me], arrived.at[me], receive.at[mine]).start()
 
@@ -267,6 +250,7 @@
         return carry
 
     lax.fori_loop(1, devices, tell, 0)
+    between()
 
     def step(turn, carry):
         group = lax.rem(mine + 2 * groups - 1 - turn, groups)
@@ -283,11 +267,9 @@
                 cells = here[device, spot : spot + 1]
                 value = arrived[device, spot : spot + 1]
             row, column = places(cells)
-            high = value.astype(jnp.bfloat16).astype(jnp.float32)
-            row_hit = hits(row, width)
-            spread = [jnp.where(row_hit, part, 0.0) for part in (high, value - high)]
-            left.append(jnp.concatenate(spread, 0).astype(jnp.bfloat16))
-            right.append(jnp.where(hits(column, width), 1.0, 0.0).astype(jnp.bfloat16))
+            row_hit = narrow_hits(row, width)
+            left.append(jnp.concatenate([jnp.where(row_hit, part, zero) for part in split(value)], 0))
+            right.append(jnp.where(narrow_hits(column, width), one, zero))
         total[...] += lax.dot_general(
             jnp.concatenate(left, 1),
             jnp.concatenate(right, 1),
@@ -301,21 +283,25 @@
 
 def phase_kernel(mode, *refs):
     first, last = mode == "first", mode == "last"
-    place_ref, weights_hbm, faces_ref, sigma_ref = refs[:4]
-    refs = refs[4:]
+    place_ref, weights_hbm, sigma_ref = refs[:3]
+    refs = refs[3:]
     if first:
-        cells_ref, value_ref, smoothed, field_out, here = refs[:5]
+        cells_ref, value_ref, stacked_ref, stacked_low, stacked_high = refs[:5]
+        smoothed, field_out, here, faces_ref = refs[5:9]
+        refs = refs[9:]
+    elif last:
+        faces_ref, here, seen_ref, base_ref, once_ref, base_seen_ref = refs[:6]
+        smoothed, increment = refs[6:8]
+        refs = refs[8:]
+    else:
+        faces_ref, here, seen_ref, smoothed, field_out = refs[:5]
         refs = refs[5:]
-    elif last:
-        here, seen_ref, base_ref, once_ref, smoothed, scale_out = refs[:6]
-        refs = refs[6:]
-    else:
-        here, seen_ref, smoothed, field_out = refs[:4]
-        refs = refs[4:]
     weights_ref, turned, weighted, parcel, arrived, total, field_ref, low, high, work = refs[:10]
     copied, send, receive, edges, edge_send, edge_receive = refs[10:16]
     refs = refs[16:]
-    if not first:
+    if first:
+        stacked_edges, stacked_send, stacked_receive = refs
+    else:
         square, found, back, found_send, found_receive = refs[:5]
         refs = refs[5:]
     if last:
@@ -332,7 +318,11 @@
     def placing(rank):
         return jnp.where(number * ranks + rank == place_ref[0:1], 1.0, 0.0)
 
+    stacked_copies = []
     if first:
+        stacked_copies = swap_edges(
+            stacked_ref, stacked_low, stacked_high, stacked_edges, stacked_send, stacked_receive
+        )
         turned[...] = value_ref[...].T
     else:
         gather_and_send(here, seen_ref, square, found, back, found_send, found_receive)
@@ -361,7 +351,14 @@
             chosen, weighted[...], precision=EXACT, preferred_element_type=jnp.float32
         )
     total[...] = jnp.zeros_like(total)
-    scatter_arrivals(first, here, parcel, arrived, total, send, receive)
+
+    def between():
+        if first:
+            for copy in stacked_copies:
+                copy.wait()
+            build_faces(stacked_ref, stacked_edges, faces_ref)
+
+    scatter_arrivals(first, here, parcel, arrived, total, send, receive, between)
 
     field = total[0:256] + total[256:512]
     levels, tile_rows, tile_columns = field_ref.shape
@@ -436,9 +433,14 @@
             rest - step * along,
             step * alpha - alpha - step * along,
         ]
-        for spot in range(4):
-            row = jnp.where(lane == spot, scales[spot], row)
-        scale_out[...] = row
+        for level in range(levels):
+            flat = slice(level * tile_rows, (level + 1) * tile_rows)
+            increment[level] = scales[0] * base_seen_ref[flat] - scales[1] * seen_ref[flat]
+            smoothed[level] = (
+                scales[2] * base_ref[level]
+                + scales[3] * once_ref[level]
+                + scales[1] * smoothed[level]
+            )
         wait_for(parts, part_send)
     else:
         wait_for(arrived.at[pl.ds(0, devices - 1)], send)
@@ -446,18 +448,20 @@
             wait_for(back.at[pl.ds(0, devices - 1)], found_send)
 
 
-def phase(mode, number, place, obs_weights, weights, sigma, *more):
+def phase(mode, number, place, obs_weights, sigma, *more):
     first, last = mode == "first", mode == "last"
     held, width = obs_weights.shape[:2]
     devices = lax.axis_size("lat") * lax.axis_size("lon")
     levels, rows, columns = sigma.shape
     real = jnp.float32
+    padded = (levels, rows + 2 * EDGE, 2 * columns)
     tile = jax.ShapeDtypeStruct(sigma.shape, real)
     flat = jax.ShapeDtypeStruct((levels * rows, columns), real)
     if first:
         outs = (tile, flat, jax.ShapeDtypeStruct((devices, 2, width), jnp.int32))
+        outs += (jax.ShapeDtypeStruct((4,) + padded, real),)
     elif last:
-        outs = (tile, jax.ShapeDtypeStruct((1, columns), real))
+        outs = (tile, tile)
     else:
         outs = (tile, flat)
     parcel = pltpu.VMEM((devices, 4 if first else 2, width), real)
@@ -472,12 +476,14 @@
         pltpu.VMEM(sigma.shape, real),
         pltpu.VMEM((levels, EDGE, rows), real),
         pltpu.VMEM((levels, EDGE, rows), real),
-        pltpu.VMEM(weights.shape[1:], real),
+        pltpu.VMEM(padded, real),
         dma,
         dma,
         dma((devices * 2 // GROUP,)),
     ] + edge_scratch(levels, columns)
-    if not first:
+    if first:
+        scratch += edge_scratch(3 * levels, columns)
+    else:
         scratch += [pltpu.VMEM((512, 256), jnp.bfloat16), parcel, parcel, dma, dma]
     if last:
         scratch += [
@@ -486,7 +492,7 @@
             dma,
             dma,
         ]
-    inputs = (place, obs_weights, weights, sigma) + more
+    inputs = (place, obs_weights, sigma) + more
     specs = [VMEM] * len(inputs)
     specs[1] = pl.BlockSpec(memory_space=pl.ANY)
     return pl.pallas_call(
@@ -508,14 +514,17 @@
     rank = jnp.sum(before.astype(jnp.int32), axis=0)
     place = jnp.stack([target * 2 + rank] * 8)
     stacked = jnp.concatenate([mask.astype(jnp.float32), east_coef, north_coef])
-    weights = faces(stacked)
-    fixed = (place, obs_weights, weights, sigma)
-    base, base_field, here = phase("first", 1, *fixed, cells, innovations)
-    once, once_field = phase("middle", 2, *fixed, here, base_field)
-    again, scale = phase("last", 3, *fixed, here, once_field, base, once)
-    scale = scale[0]
-    increment = (scale[0] * base_field - scale[1] * once_field).reshape(sigma.shape)
-    residual = scale[2] * base + scale[3] * once + scale[1] * again
+    columns = stacked.shape[2]
+    low = jnp.swapaxes(stacked[:, :, :EDGE], 1, 2)
+    high = jnp.swapaxes(stacked[:, :, columns - EDGE :], 1, 2)
+    fixed = (place, obs_weights, sigma)
+    base, base_field, here, weights = phase(
+        "first", 1, *fixed, cells, innovations, stacked, low, high
+    )
+    once, once_field = phase("middle", 2, *fixed, weights, here, base_field)
+    residual, increment = phase(
+        "last", 3, *fixed, weights, here, once_field, base, once, base_field
+    )
     return (increment, residual)
 
 

time: 205 us -> 175 us (0.85)
  Pallas kernels: 193 us -> 165 us
  other arithmetic: 6.2 us -> 1.56 us
  local copies, waits for them, and re-layouts: 4.2 us -> 7.55 us
    pallas_call x1 -> x0, Pallas kernels: 14.8 us -> none  [faces(): pl.pallas_call(faces_kernel, out_shape=jax.ShapeDtypeStruct((4, levels //...]
    pallas_call x3, Pallas kernels: 178 us -> 165 us  [phase(): pl.pallas_call(functools.partial(phase_kernel, mode), out_shape=outs, in_...]
    unnamed x9 -> x11, local copies, waits for them, and re-layouts: 3.25 us -> 7.27 us
    add x1 -> x0, other arithmetic: 2.64 us -> none  [body(): residual = scale[2] * base + scale[3] * once + scale[1] * again]
where the time goes in v2:
time: 175 us; the launch traced here: 174 us
  Pallas kernels  165 us (94%)
  local copies, waits for them, and re-layouts  7.55 us (4%)
    pallas_call x3, Pallas kernels, phase(): pl.pallas_call(functools.partial(phase_kernel, mode), out_shape=outs, in_...  165 us
    unnamed x11, local copies, waits for them, and re-layouts  7.27 us

profile of v2, /device:TPU:1, one launch (start us, length us, event | category | flops | bytes accessed | tf_op | source)
XLA Modules:
  0.0 174.5 jit_solution(14675627324067887229)
XLA Ops:
  0.6 0.8 convert_reduce_fusion
  1.5 0.7 multiply_add_fusion
  2.1 1.1 copy.15
  3.2 1.1 copy.16
  4.3 1.1 copy.14
  5.4 0.1 pad_maximum_fusion
  5.5 0.3 copy.17.refs_5_
  5.8 0.0 copy-start
  5.8 0.9 copy-done
  6.7 0.0 copy-start.1
  6.7 0.8 copy-done.1
  7.6 0.0 copy-start.2
  7.6 0.8 copy-done.2
  8.4 47.9 %first.1 = (f32[4,128,128]{2,1,0:T(8,128)S(1)}, f32[512,128]{1,0:T(8,128)S(1)}, s32[128,2,128]{2,1,0:T(2,128)S(1)}, f32[4,4,160,256]{3,2,1,0:T(8,128)S(1)}) custom-call(s32[8,128]{1,0:T(8,128)S(1)} %stack.2.refs_0_, f32[128,128,128]{2,1,0:T(8,128)} %refs_1_.5, f32[4,128,128]{2,1,0:T(8,128)S(1)} %copy-done, s32[128,128]{1,0:T(8,128)S(1)} %copy-done.1, ...), custom_call_target="tpu_custom_call" | custom-call | tf_op jit(solution)/shard_map/first/pallas_call | solution.py:498
  56.3 56.7 %middle.1 = (f32[4,128,128]{2,1,0:T(8,128)S(1)}, f32[512,128]{1,0:T(8,128)S(1)}) custom-call(s32[8,128]{1,0:T(8,128)S(1)} %stack.2.refs_0_, f32[128,128,128]{2,1,0:T(8,128)} %refs_1_.5, f32[4,128,128]{2,1,0:T(8,128)S(1)} %copy-done, f32[4,4,160,256]{3,2,1,0:T(8,128)S(1)} %get-tuple-element.10.refs_3_, s32[128,2,128]{2,1,0:T(2,128)S(1)} %get-tuple-element.11.refs_4_, ...), custom_call_target="tpu_custom_call" | custom-call | tf_op jit(solution)/shard_map/middle/pallas_call | solution.py:498
  112.9 60.2 %last.1 = (f32[4,128,128]{2,1,0:T(8,128)S(1)}, f32[4,128,128]{2,1,0:T(8,128)S(1)}) custom-call(s32[8,128]{1,0:T(8,128)S(1)} %stack.2.refs_0_, f32[128,128,128]{2,1,0:T(8,128)} %refs_1_.5, f32[4,128,128]{2,1,0:T(8,128)S(1)} %copy-done, f32[4,4,160,256]{3,2,1,0:T(8,128)S(1)} %get-tuple-element.10.refs_3_, s32[128,2,128]{2,1,0:T(2,128)S(1)} %get-tuple-element.11.refs_4_, ...), custom_call_target="tpu_custom_call" | custom-call | tf_op jit(solution)/shard_map/last/pallas_call | solution.py:498
  173.1 0.7 copy.20
  173.8 0.7 copy.21
  (3 shorter events, 0.0 us)
Async XLA Ops:
  5.8 1.0 copy-start
  6.7 0.8 copy-start.1
  7.6 0.8 copy-start.2

commit v3 on v2

--- a/solution.py
+++ b/solution.py
@@ -143,7 +143,7 @@
         return carry
 
     lax.fori_loop(1, devices, greet, 0)
-    pl.semaphore_wait(barrier, devices - 1)
+    return barrier
 
 
 def push(source, target, send, receive, device):
@@ -281,35 +281,20 @@
     lax.fori_loop(0, groups, step, 0)
 
 
-def phase_kernel(mode, *refs):
+def phase(mode, place_ref, weights_ref, sigma_ref, faces_ref, here, common, sparse, more):
     first, last = mode == "first", mode == "last"
-    place_ref, weights_hbm, sigma_ref = refs[:3]
-    refs = refs[3:]
+    turned, weighted, total, field_ref, low, high, work = common[:7]
+    send, receive, edges, edge_send, edge_receive = common[7:12]
+    parcel, arrived = sparse[:2]
     if first:
-        cells_ref, value_ref, stacked_ref, stacked_low, stacked_high = refs[:5]
-        smoothed, field_out, here, faces_ref = refs[5:9]
-        refs = refs[9:]
-    elif last:
-        faces_ref, here, seen_ref, base_ref, once_ref, base_seen_ref = refs[:6]
-        smoothed, increment = refs[6:8]
-        refs = refs[8:]
+        cells_ref, value_ref, ready, smoothed, field_out, stacked = more
     else:
-        faces_ref, here, seen_ref, smoothed, field_out = refs[:5]
-        refs = refs[5:]
-    weights_ref, turned, weighted, parcel, arrived, total, field_ref, low, high, work = refs[:10]
-    copied, send, receive, edges, edge_send, edge_receive = refs[10:16]
-    refs = refs[16:]
-    if first:
-        stacked_edges, stacked_send, stacked_receive = refs
-    else:
-        square, found, back, found_send, found_receive = refs[:5]
-        refs = refs[5:]
+        square, found, back, found_send, found_receive = sparse[2:]
     if last:
-        part, parts, part_send, part_receive = refs
-
-    load = pltpu.make_async_copy(weights_hbm, weights_ref, copied)
-    load.start()
-    greet_everyone()
+        seen_ref, base_ref, once_ref, base_seen_ref, smoothed, increment = more[:6]
+        part, parts, part_send, part_receive = more[6:]
+    elif not first:
+        seen_ref, smoothed, field_out = more
     devices, me = everyone()
     ranks, width = here.shape[1:]
     held = turned.shape[1]
@@ -320,9 +305,7 @@
 
     stacked_copies = []
     if first:
-        stacked_copies = swap_edges(
-            stacked_ref, stacked_low, stacked_high, stacked_edges, stacked_send, stacked_receive
-        )
+        stacked_copies = swap_edges(*stacked)
         turned[...] = value_ref[...].T
     else:
         gather_and_send(here, seen_ref, square, found, back, found_send, found_receive)
@@ -336,7 +319,8 @@
             )
             for rank in range(ranks)
         )
-    load.wait()
+    if first:
+        ready()
     weigh(turned, weights_ref, weighted)
     for rank in range(ranks):
         chosen = placing(rank)
@@ -356,7 +340,7 @@
         if first:
             for copy in stacked_copies:
                 copy.wait()
-            build_faces(stacked_ref, stacked_edges, faces_ref)
+            build_faces(stacked[0], stacked[3], faces_ref)
 
     scatter_arrivals(first, here, parcel, arrived, total, send, receive, between)
 
@@ -448,84 +432,89 @@
             wait_for(back.at[pl.ds(0, devices - 1)], found_send)
 
 
-def phase(mode, number, place, obs_weights, sigma, *more):
-    first, last = mode == "first", mode == "last"
-    held, width = obs_weights.shape[:2]
+def kernel(*refs):
+    place_ref, weights_hbm, sigma_ref, cells_ref, value_ref, mask_ref, east_ref, north_ref = refs[:8]
+    increment, residual = refs[8:10]
+    base, once, base_field, once_field, here, faces_ref, weights_ref, copied = refs[10:18]
+    common, wide, narrow = refs[18:30], refs[30:32], refs[32:39]
+    stacked, finish = refs[39:45], refs[45:]
+    load = pltpu.make_async_copy(weights_hbm, weights_ref, copied)
+    load.start()
+    barrier = greet_everyone()
+    fields, low, high = stacked[:3]
+    levels, rows, columns = sigma_ref.shape
+    for kind, ref in enumerate((mask_ref, east_ref, north_ref)):
+        for level in range(levels):
+            tile = ref[level].astype(jnp.float32)
+            flat = tile.T
+            fields[kind * levels + level] = tile
+            low[kind * levels + level] = flat[0:EDGE]
+            high[kind * levels + level] = flat[columns - EDGE :]
+    pl.semaphore_wait(barrier, everyone()[0] - 1)
+    fixed = (place_ref, weights_ref, sigma_ref, faces_ref, here, common)
+    phase("first", *fixed, wide, (cells_ref, value_ref, load.wait, base, base_field, stacked))
+    phase("middle", *fixed, narrow, (base_field, once, once_field))
+    phase(
+        "last",
+        *fixed,
+        narrow,
+        (once_field, base, once, base_field, residual, increment) + finish,
+    )
+
+
+def body(sigma, east_coef, north_coef, mask, innovations, cells, owner, obs_weights):
+    held, width = cells.shape
     devices = lax.axis_size("lat") * lax.axis_size("lon")
     levels, rows, columns = sigma.shape
-    real = jnp.float32
-    padded = (levels, rows + 2 * EDGE, 2 * columns)
-    tile = jax.ShapeDtypeStruct(sigma.shape, real)
-    flat = jax.ShapeDtypeStruct((levels * rows, columns), real)
-    if first:
-        outs = (tile, flat, jax.ShapeDtypeStruct((devices, 2, width), jnp.int32))
-        outs += (jax.ShapeDtypeStruct((4,) + padded, real),)
-    elif last:
-        outs = (tile, tile)
-    else:
-        outs = (tile, flat)
-    parcel = pltpu.VMEM((devices, 4 if first else 2, width), real)
-    dma = pltpu.SemaphoreType.DMA
-    scratch = [
-        pltpu.VMEM(obs_weights.shape, real),
-        pltpu.VMEM((width, held), real),
-        pltpu.VMEM((held, width), real),
-        parcel,
-        parcel,
-        pltpu.VMEM((512, 256), real),
-        pltpu.VMEM(sigma.shape, real),
-        pltpu.VMEM((levels, EDGE, rows), real),
-        pltpu.VMEM((levels, EDGE, rows), real),
-        pltpu.VMEM(padded, real),
-        dma,
-        dma,
-        dma((devices * 2 // GROUP,)),
-    ] + edge_scratch(levels, columns)
-    if first:
-        scratch += edge_scratch(3 * levels, columns)
-    else:
-        scratch += [pltpu.VMEM((512, 256), jnp.bfloat16), parcel, parcel, dma, dma]
-    if last:
-        scratch += [
-            pltpu.VMEM((1, columns), real),
-            pltpu.VMEM((devices - 1, 1, columns), real),
-            dma,
-            dma,
-        ]
-    inputs = (place, obs_weights, sigma) + more
-    specs = [VMEM] * len(inputs)
-    specs[1] = pl.BlockSpec(memory_space=pl.ANY)
-    return pl.pallas_call(
-        functools.partial(phase_kernel, mode),
-        out_shape=outs,
-        in_specs=specs,
-        out_specs=(VMEM,) * len(outs),
-        scratch_shapes=scratch,
-        compiler_params=remote(number),
-        name=mode,
-    )(*inputs)
-
-
-def body(sigma, east_coef, north_coef, mask, innovations, cells, owner, obs_weights):
-    held = cells.shape[0]
     target = owner[:, 0]
     order = jnp.arange(held, dtype=jnp.int32)
     before = (target[:, None] == target[None, :]) & (order[:, None] < order[None, :])
     rank = jnp.sum(before.astype(jnp.int32), axis=0)
     place = jnp.stack([target * 2 + rank] * 8)
-    stacked = jnp.concatenate([mask.astype(jnp.float32), east_coef, north_coef])
-    columns = stacked.shape[2]
-    low = jnp.swapaxes(stacked[:, :, :EDGE], 1, 2)
-    high = jnp.swapaxes(stacked[:, :, columns - EDGE :], 1, 2)
-    fixed = (place, obs_weights, sigma)
-    base, base_field, here, weights = phase(
-        "first", 1, *fixed, cells, innovations, stacked, low, high
-    )
-    once, once_field = phase("middle", 2, *fixed, weights, here, base_field)
-    residual, increment = phase(
-        "last", 3, *fixed, weights, here, once_field, base, once, base_field
-    )
-    return (increment, residual)
+    real = jnp.float32
+    dma = pltpu.SemaphoreType.DMA
+    padded = (levels, rows + 2 * EDGE, 2 * columns)
+    tile = pltpu.VMEM(sigma.shape, real)
+    flat = pltpu.VMEM((levels * rows, columns), real)
+    parcel = pltpu.VMEM((devices, 2, width), real)
+    twice = pltpu.VMEM((devices, 4, width), real)
+    strip = pltpu.VMEM((levels, EDGE, rows), real)
+    strips = pltpu.VMEM((3 * levels, EDGE, rows), real)
+    scratch = [tile, tile, flat, flat, pltpu.VMEM((devices, 2, width), jnp.int32)]
+    scratch += [pltpu.VMEM((4,) + padded, real), pltpu.VMEM(obs_weights.shape, real), dma]
+    scratch += [
+        pltpu.VMEM((width, held), real),
+        pltpu.VMEM((held, width), real),
+        pltpu.VMEM((512, 256), real),
+        tile,
+        strip,
+        strip,
+        pltpu.VMEM(padded, real),
+        dma,
+        dma((devices * 2 // GROUP,)),
+    ] + edge_scratch(levels, columns)
+    scratch += [twice, twice]
+    scratch += [parcel, parcel, pltpu.VMEM((512, 256), jnp.bfloat16), parcel, parcel, dma, dma]
+    scratch += [pltpu.VMEM((3 * levels, rows, columns), real), strips, strips]
+    scratch += edge_scratch(3 * levels, columns)
+    scratch += [
+        pltpu.VMEM((1, columns), real),
+        pltpu.VMEM((devices - 1, 1, columns), real),
+        dma,
+        dma,
+    ]
+    specs = [VMEM] * 8
+    specs[1] = pl.BlockSpec(memory_space=pl.ANY)
+    out = jax.ShapeDtypeStruct(sigma.shape, real)
+    return pl.pallas_call(
+        kernel,
+        out_shape=(out, out),
+        in_specs=specs,
+        out_specs=(VMEM, VMEM),
+        scratch_shapes=scratch,
+        compiler_params=remote(1),
+        name="whole",
+    )(place, obs_weights, sigma, cells, innovations, mask, east_coef, north_coef)
 
 
 def solution(mesh):

time: 175 us -> 162 us (0.926)
  Pallas kernels: 165 us -> 153 us
    pallas_call x3 -> x1, Pallas kernels: 165 us -> 153 us  [body(): pl.pallas_call(kernel, out_shape=(out, out), in_specs=specs, out_specs=(V...]
    unnamed x11 -> x14, local copies, waits for them, and re-layouts: 7.27 us -> 6.88 us
where the time goes in v3:
time: 162 us
  Pallas kernels  153 us (94%)
  local copies, waits for them, and re-layouts  6.89 us (4%)
    pallas_call x1, Pallas kernels, body(): pl.pallas_call(kernel, out_shape=(out, out), in_specs=specs, out_specs=(V...  153 us
    unnamed x14, local copies, waits for them, and re-layouts  6.88 us

profile of v3, /device:TPU:1, one launch (start us, length us, event | category | flops | bytes accessed | tf_op | source)
XLA Modules:
  0.0 161.6 jit_solution(11232216290111299627)
XLA Ops:
  0.6 0.8 convert_reduce_fusion
  1.5 0.7 multiply_add_fusion
  2.1 0.0 copy-start
  2.1 0.9 copy-done
  3.1 0.0 copy-start.1
  3.1 0.9 copy-done.1
  4.0 0.0 copy-start.2
  4.0 0.9 copy-done.2
  5.0 0.0 copy-start.3
  5.0 0.9 copy-done.3
  5.9 0.0 copy-start.4
  5.9 0.8 copy-done.4
  6.8 0.0 copy-start.5
  6.8 0.8 copy-done.5
  7.6 152.6 %whole.1 = (f32[4,128,128]{2,1,0:T(8,128)S(1)}, f32[4,128,128]{2,1,0:T(8,128)S(1)}) custom-call(s32[8,128]{1,0:T(8,128)S(1)} %stack.2.refs_0_, f32[128,128,128]{2,1,0:T(8,128)} %refs_1_.1, f32[4,128,128]{2,1,0:T(8,128)S(1)} %copy-done, s32[128,128]{1,0:T(8,128)S(1)} %copy-done.4, f32[128,128]{1,0:T(8,128)S(1)} %copy-done.5, s32[4,128,128]{2,1,0:T(8,128)S(1)} %copy-done.1, ...), custom_call_target="tpu_custom_call" | custom-call | tf_op jit(solution)/shard_map/whole/pallas_call | solution.py:509
  160.2 0.7 copy.12
  160.9 0.7 copy.13
  (1 shorter events, 0.0 us)
Async XLA Ops:
  2.1 0.9 copy-start
  3.1 0.9 copy-start.1
  4.0 0.9 copy-start.2
  5.0 0.9 copy-start.3
  5.9 0.8 copy-start.4
  6.8 0.8 copy-start.5

commit v4 on v3

--- a/solution.py
+++ b/solution.py
@@ -9,7 +9,7 @@
 
 PASSES = 5
 EDGE = 16
-GROUP = 16
+GROUP = 32
 STEP = 16
 MESH = pl.DeviceIdType.MESH
 EXACT = lax.Precision.HIGHEST

time: 162 us -> 154 us (0.951)
  Pallas kernels: 153 us -> 145 us
    pallas_call x1, Pallas kernels: 153 us -> 145 us  [body(): pl.pallas_call(kernel, out_shape=(out, out), in_specs=specs, out_specs=(V...]
where the time goes in v4:
time: 154 us
  Pallas kernels  145 us (94%)
  local copies, waits for them, and re-layouts  6.89 us (4%)
    pallas_call x1, Pallas kernels, body(): pl.pallas_call(kernel, out_shape=(out, out), in_specs=specs, out_specs=(V...  145 us
    unnamed x14, local copies, waits for them, and re-layouts  6.88 us

profile of v4, /device:TPU:1, one launch (start us, length us, event | category | flops | bytes accessed | tf_op | source)
XLA Modules:
  0.0 154.1 jit_solution(16455319831969042704)
XLA Ops:
  0.6 0.8 convert_reduce_fusion
  1.5 0.7 multiply_add_fusion
  2.1 0.0 copy-start
  2.1 0.9 copy-done
  3.1 0.0 copy-start.1
  3.1 0.9 copy-done.1
  4.0 0.0 copy-start.2
  4.0 0.9 copy-done.2
  5.0 0.0 copy-start.3
  5.0 0.9 copy-done.3
  5.9 0.0 copy-start.4
  5.9 0.8 copy-done.4
  6.8 0.0 copy-start.5
  6.8 0.8 copy-done.5
  7.6 145.1 %whole.1 = (f32[4,128,128]{2,1,0:T(8,128)S(1)}, f32[4,128,128]{2,1,0:T(8,128)S(1)}) custom-call(s32[8,128]{1,0:T(8,128)S(1)} %stack.2.refs_0_, f32[128,128,128]{2,1,0:T(8,128)} %refs_1_.1, f32[4,128,128]{2,1,0:T(8,128)S(1)} %copy-done, s32[128,128]{1,0:T(8,128)S(1)} %copy-done.4, f32[128,128]{1,0:T(8,128)S(1)} %copy-done.5, s32[4,128,128]{2,1,0:T(8,128)S(1)} %copy-done.1, ...), custom_call_target="tpu_custom_call" | custom-call | tf_op jit(solution)/shard_map/whole/pallas_call | solution.py:509
  152.7 0.7 copy.12
  153.4 0.7 copy.13
  (1 shorter events, 0.0 us)
Async XLA Ops:
  2.1 0.9 copy-start
  3.1 0.9 copy-start.1
  4.0 0.9 copy-start.2
  5.0 0.9 copy-start.3
  5.9 0.8 copy-start.4
  6.8 0.8 copy-start.5
